TPU v7x, 32 devices: a whole 2x2x4 slice. The times are simulated.
32 devices in a mesh: seq: 4 (over x, core), fsdp: 8 (over z, y).
Axes of the slice: x: 2, y: 2, z: 4, core: 2. Of those that a mesh axis runs over, the one named last changes fastest.
Arguments:
- image_tokens: bfloat16 [8, 1024, 1536], P('fsdp', 'seq'), may hold values from -6 to 6
- text_tokens: bfloat16 [8, 160, 1536], P('fsdp', 'seq'), may hold values from -6 to 6
- condition: bfloat16 [8, 1536], P('fsdp'), may hold values from -6 to 6
- occupied: int32 [8], P('fsdp'), may hold values 0 or 1
- image_cotangent: bfloat16 [8, 1024, 1536], P('fsdp', 'seq'), may hold values from -6 to 6
- text_cotangent: bfloat16 [8, 160, 1536], P('fsdp', 'seq'), may hold values from -6 to 6
- image_modulator: bfloat16 [1, 1536, 9216], P(None, 'fsdp'), may hold values from -0.15625 to 0.15625
- image_heads: bfloat16 [1, 1536, 4608], P(None, 'fsdp'), may hold values from -0.21875 to 0.21875
- image_merge: bfloat16 [1, 1536, 1536], P(None, 'fsdp'), may hold values from -0.3125 to 0.3125
- image_expand: bfloat16 [1, 1536, 6144], P(None, 'fsdp'), may hold values from -0.15625 to 0.15625
- image_reduce: bfloat16 [1, 6144, 1536], P(None, 'fsdp'), may hold values from -0.078125 to 0.078125
- text_modulator: bfloat16 [1, 1536, 9216], P(None, 'fsdp'), may hold values from -0.15625 to 0.15625
- text_heads: bfloat16 [1, 1536, 4608], P(None, 'fsdp'), may hold values from -0.21875 to 0.21875
- text_merge: bfloat16 [1, 1536, 1536], P(None, 'fsdp'), may hold values from -0.3125 to 0.3125
- text_expand: bfloat16 [1, 1536, 6144], P(None, 'fsdp'), may hold values from -0.15625 to 0.15625
- text_reduce: bfloat16 [1, 6144, 1536], P(None, 'fsdp'), may hold values from -0.078125 to 0.078125
Outputs:
- image_output: bfloat16 [8, 1024, 1536], P('fsdp', 'seq')
- text_output: bfloat16 [8, 160, 1536], P('fsdp', 'seq')
- image_input_grad: bfloat16 [8, 1024, 1536], P('fsdp', 'seq')
- text_input_grad: bfloat16 [8, 160, 1536], P('fsdp', 'seq')
- condition_grad: float32 [8, 1536], P('fsdp')
- image_modulator_grad: float32 [1, 1536, 9216], P(None, 'fsdp')
- image_heads_grad: float32 [1, 1536, 4608], P(None, 'fsdp')
- image_merge_grad: float32 [1, 1536, 1536], P(None, 'fsdp')
- image_expand_grad: float32 [1, 1536, 6144], P(None, 'fsdp')
- image_reduce_grad: float32 [1, 6144, 1536], P(None, 'fsdp')
- text_modulator_grad: float32 [1, 1536, 9216], P(None, 'fsdp')
- text_heads_grad: float32 [1, 1536, 4608], P(None, 'fsdp')
- text_merge_grad: float32 [1, 1536, 1536], P(None, 'fsdp')
- text_expand_grad: float32 [1, 1536, 6144], P(None, 'fsdp')
- text_reduce_grad: float32 [1, 6144, 1536], P(None, 'fsdp')
All inputs are finite; a program needn't handle non-finite values. No bound on the sum of `occupied` on one device may be relied on, other than what follows from the above.
Results may differ from a plain program's by a relative error of at most 0.02.
The roundings to bfloat16 on the way count: a program that leaves them out, or rounds other values in their place, can miss the bound.
Values may be sent and summed in bfloat16 or wider, within the bound.
No kernel may reach another device: no remote copies, remote signals or barrier semaphores. Data moves between devices by JAX's collectives and lax.ppermute only.
A program may use at most 448 MiB of HBM per device.

v0:
```python
import jax
import jax.numpy as jnp
from jax import lax
from jax.sharding import PartitionSpec as P

HEAD_DIM = 64
EPSILON = 1e-06


def layer_norm(values):
    centered = values - jnp.mean(values, axis=-1, keepdims=True)
    inverse = lax.rsqrt(jnp.mean(centered * centered, axis=-1, keepdims=True) + EPSILON)
    return (centered * inverse, inverse)


def norm_back(incoming, normed, inverse):
    mean_plain = jnp.mean(incoming, axis=-1, keepdims=True)
    mean_mixed = jnp.mean(incoming * normed, axis=-1, keepdims=True)
    return inverse * (incoming - mean_plain - normed * mean_mixed)


def product(former, latter):
    return jnp.dot(former, latter, preferred_element_type=jnp.float32)


def product_nt(former, latter):
    return lax.dot_general(
        former, latter, (((1,), (1,)), ((), ())), preferred_element_type=jnp.float32
    )


def product_tn(former, latter):
    return lax.dot_general(
        former, latter, (((0,), (0,)), ((), ())), preferred_element_type=jnp.float32
    )


def gelu_tanh(values):
    return jax.nn.gelu(values, approximate=True)


def reduce_rows(former, latter):
    return lax.psum_scatter(
        product_tn(former, latter).astype(jnp.bfloat16), "fsdp", scatter_dimension=0, tiled=True
    ).astype(jnp.float32)


def collect(weights, layer_index):
    return (
        lax.all_gather(weights[0][layer_index], "fsdp", axis=0, tiled=True),
        lax.all_gather(weights[1][layer_index], "fsdp", axis=0, tiled=True),
        lax.all_gather(weights[2][layer_index], "fsdp", axis=0, tiled=True),
        lax.all_gather(weights[3][layer_index], "fsdp", axis=0, tiled=True),
        lax.all_gather(weights[4][layer_index], "fsdp", axis=0, tiled=True),
        lax.all_gather(weights[5][layer_index], "fsdp", axis=0, tiled=True),
        lax.all_gather(weights[6][layer_index], "fsdp", axis=0, tiled=True),
        lax.all_gather(weights[7][layer_index], "fsdp", axis=0, tiled=True),
    )


def head_forward(items):
    query_head, key_head, value_head = items
    scores = product_nt(query_head, key_head) * HEAD_DIM ** (-0.5)
    highest = jnp.max(scores, axis=-1, keepdims=True)
    exponent = jnp.exp(scores - highest)
    totals = jnp.sum(exponent, axis=-1, keepdims=True)
    logsum = highest + jnp.log(totals)
    output = product((exponent / totals).astype(jnp.bfloat16), value_head).astype(jnp.bfloat16)
    return (output, logsum)


def head_backward(items):
    query_head, key_head, value_head, output_grad, logsum = items
    score_scale = HEAD_DIM ** (-0.5)
    scores = product_nt(query_head, key_head) * score_scale
    probs = jnp.exp(scores - logsum)
    probs_grad = product_nt(output_grad, value_head)
    value_grad = product_tn(probs.astype(jnp.bfloat16), output_grad)
    scores_grad = (
        probs * (probs_grad - jnp.sum(probs * probs_grad, axis=-1, keepdims=True))
    ).astype(jnp.bfloat16)
    query_grad = product(scores_grad, key_head) * score_scale
    key_grad = product_tn(scores_grad, query_head) * score_scale
    return (query_grad, key_grad, value_grad)


def per_device(
    image_tokens,
    text_tokens,
    condition,
    occupied,
    image_cotangent,
    text_cotangent,
    image_modulator,
    image_heads,
    image_merge,
    image_expand,
    image_reduce,
    text_modulator,
    text_heads,
    text_merge,
    text_expand,
    text_reduce,
):
    splits = lax.axis_size("seq")
    layers = image_heads.shape[0]
    model_width = condition.shape[1]
    image_count = image_tokens.shape[1]
    token_count = image_count + text_tokens.shape[1]
    head_slab = model_width // splits
    local_heads = head_slab // HEAD_DIM
    occupancy = occupied.astype(jnp.float32)[0]
    weights = (
        image_heads,
        image_merge,
        image_expand,
        image_reduce,
        text_heads,
        text_merge,
        text_expand,
        text_reduce,
    )
    condition_value = condition.astype(jnp.float32)
    condition_act = jax.nn.silu(condition_value).astype(jnp.bfloat16)
    every_condition = lax.all_gather(condition_act, "fsdp", axis=0, tiled=True)
    own_width = image_modulator.shape[1]
    own_first = lax.axis_index("fsdp") * own_width
    condition_slice = lax.dynamic_slice_in_dim(every_condition, own_first, own_width, 1)
    image_part = jnp.einsum(
        "fr,lrk->flk", condition_slice, image_modulator, preferred_element_type=jnp.float32
    )
    text_part = jnp.einsum(
        "fr,lrk->flk", condition_slice, text_modulator, preferred_element_type=jnp.float32
    )
    image_mod, text_mod = (
        lax.psum_scatter(image_part, "fsdp", scatter_dimension=0, tiled=True),
        lax.psum_scatter(text_part, "fsdp", scatter_dimension=0, tiled=True),
    )
    modulation = (image_mod[0], text_mod[0])
    hidden = [image_tokens[0].astype(jnp.float32), text_tokens[0].astype(jnp.float32)]
    layer_index = 0
    gathered = collect(weights, layer_index)
    portions = [jnp.split(modulation[stream][layer_index], 6) for stream in range(2)]
    first_norm = [layer_norm(hidden[stream]) for stream in range(2)]
    entries = [
        (first_norm[stream][0] * (1.0 + portions[stream][1]) + portions[stream][0]).astype(
            jnp.bfloat16
        )
        for stream in range(2)
    ]
    projected = jnp.concatenate(
        [
            product(entries[stream], gathered[4 * stream]).astype(jnp.bfloat16)
            for stream in range(2)
        ],
        0,
    )
    regrouped = lax.all_to_all(
        projected.reshape(token_count, 3, splits, head_slab),
        "seq",
        split_axis=2,
        concat_axis=0,
        tiled=True,
    )
    regrouped = regrouped.reshape(splits * token_count, 3, local_heads, HEAD_DIM)
    queries = jnp.moveaxis(regrouped[:, 0], 1, 0)
    all_keys = jnp.moveaxis(regrouped[:, 1], 1, 0)
    all_values = jnp.moveaxis(regrouped[:, 2], 1, 0)
    head_outputs, logsum = lax.map(head_forward, (queries, all_keys, all_values))
    attended = jnp.moveaxis(head_outputs, 0, 1)
    returned = lax.all_to_all(
        attended.reshape(splits * token_count, 1, head_slab),
        "seq",
        split_axis=0,
        concat_axis=1,
        tiled=True,
    )
    returned = returned.reshape(token_count, model_width)
    pieces = (returned[:image_count], returned[image_count:])
    stream_records = []
    for stream in range(2):
        portion = portions[stream]
        branch = product(pieces[stream], gathered[4 * stream + 1])
        middle = hidden[stream] + portion[2] * branch
        second_norm, second_inverse = layer_norm(middle)
        entry_mlp = (second_norm * (1.0 + portion[4]) + portion[3]).astype(jnp.bfloat16)
        pre_gelu = product(entry_mlp, gathered[4 * stream + 2])
        active = gelu_tanh(pre_gelu).astype(jnp.bfloat16)
        final_out = product(active, gathered[4 * stream + 3])
        hidden[stream] = middle + portion[5] * final_out
        stream_records.append(
            (
                first_norm[stream][0],
                first_norm[stream][1],
                entries[stream],
                pieces[stream],
                branch,
                second_norm,
                second_inverse,
                entry_mlp,
                pre_gelu,
                active,
                final_out,
            )
        )
    records = [(stream_records, queries, all_keys, all_values, logsum)]
    flowing = [
        image_cotangent[0].astype(jnp.float32) * occupancy,
        text_cotangent[0].astype(jnp.float32) * occupancy,
    ]
    mod_grads = [None] * layers
    weight_grads = [None] * layers
    for layer_index in reversed(range(layers)):
        gathered = collect(weights, layer_index)
        stream_records, queries, all_keys, all_values, logsum = records[layer_index]
        portions = [jnp.split(modulation[stream][layer_index], 6) for stream in range(2)]
        terms = [None] * 8
        middle_grads = []
        back_pieces = []
        partial_mods = []
        for stream in range(2):
            (
                normed,
                inverse,
                entry,
                piece,
                branch,
                second_norm,
                second_inverse,
                entry_mlp,
                pre_gelu,
                active,
                final_out,
            ) = stream_records[stream]
            portion = portions[stream]
            outer_grad = flowing[stream]
            gate_two = jnp.sum(outer_grad * final_out, axis=0)
            final_grad = (outer_grad * portion[5]).astype(jnp.bfloat16)
            terms[4 * stream + 3] = reduce_rows(active, final_grad)
            active_grad = product_nt(final_grad, gathered[4 * stream + 3])
            pre_grad = jax.vjp(gelu_tanh, pre_gelu)[1](active_grad)[0].astype(jnp.bfloat16)
            terms[4 * stream + 2] = reduce_rows(entry_mlp, pre_grad)
            entry_grad = product_nt(pre_grad, gathered[4 * stream + 2])
            scale_two = jnp.sum(entry_grad * second_norm, axis=0)
            shift_two = jnp.sum(entry_grad, axis=0)
            middle_grad = outer_grad + norm_back(
                entry_grad * (1.0 + portion[4]), second_norm, second_inverse
            )
            gate_one = jnp.sum(middle_grad * branch, axis=0)
            branch_grad = (middle_grad * portion[2]).astype(jnp.bfloat16)
            terms[4 * stream + 1] = reduce_rows(piece, branch_grad)
            back_pieces.append(
                product_nt(branch_grad, gathered[4 * stream + 1]).astype(jnp.bfloat16)
            )
            middle_grads.append(middle_grad)
            partial_mods.append((gate_one, shift_two, scale_two, gate_two))
        joined_grad = jnp.concatenate(back_pieces, 0).reshape(token_count, splits, head_slab)
        attended_grad = lax.all_to_all(joined_grad, "seq", split_axis=1, concat_axis=0, tiled=True)
        attended_grad = jnp.moveaxis(
            attended_grad.reshape(splits * token_count, local_heads, HEAD_DIM), 1, 0
        )
        queries_grad, keys_grad, values_grad = lax.map(
            head_backward, (queries, all_keys, all_values, attended_grad, logsum)
        )
        stacked = jnp.stack([queries_grad, keys_grad, values_grad], axis=0).astype(jnp.bfloat16)
        stacked = jnp.transpose(stacked, (2, 0, 1, 3)).reshape(
            splits * token_count, 3, 1, head_slab
        )
        projected_grad = lax.all_to_all(
            stacked, "seq", split_axis=0, concat_axis=2, tiled=True
        ).reshape(token_count, 3 * model_width)
        row_parts = (projected_grad[:image_count], projected_grad[image_count:])
        layer_mods = []
        for stream in range(2):
            normed, inverse, entry = (
                stream_records[stream][0],
                stream_records[stream][1],
                stream_records[stream][2],
            )
            portion = portions[stream]
            terms[4 * stream] = reduce_rows(entry, row_parts[stream])
            entry_grad = product_nt(row_parts[stream], gathered[4 * stream])
            scale_one = jnp.sum(entry_grad * normed, axis=0)
            shift_one = jnp.sum(entry_grad, axis=0)
            flowing[stream] = middle_grads[stream] + norm_back(
                entry_grad * (1.0 + portion[1]), normed, inverse
            )
            gate_one, shift_two, scale_two, gate_two = partial_mods[stream]
            layer_mods.append(
                jnp.concatenate([shift_one, scale_one, gate_one, shift_two, scale_two, gate_two])
            )
        mod_grads[layer_index] = layer_mods
        weight_grads[layer_index] = (
            lax.psum(terms[0].astype(jnp.bfloat16), "seq").astype(jnp.float32),
            lax.psum(terms[1].astype(jnp.bfloat16), "seq").astype(jnp.float32),
            lax.psum(terms[2].astype(jnp.bfloat16), "seq").astype(jnp.float32),
            lax.psum(terms[3].astype(jnp.bfloat16), "seq").astype(jnp.float32),
            lax.psum(terms[4].astype(jnp.bfloat16), "seq").astype(jnp.float32),
            lax.psum(terms[5].astype(jnp.bfloat16), "seq").astype(jnp.float32),
            lax.psum(terms[6].astype(jnp.bfloat16), "seq").astype(jnp.float32),
            lax.psum(terms[7].astype(jnp.bfloat16), "seq").astype(jnp.float32),
        )
    image_mod_grad = jnp.stack([mod_grads[0][0]])[None]
    text_mod_grad = jnp.stack([mod_grads[0][1]])[None]
    image_mod_total, text_mod_total = (
        lax.psum(image_mod_grad.astype(jnp.bfloat16), "seq").astype(jnp.float32),
        lax.psum(text_mod_grad.astype(jnp.bfloat16), "seq").astype(jnp.float32),
    )
    image_every, text_every = (
        lax.all_gather(image_mod_total.astype(jnp.bfloat16), "fsdp", axis=0, tiled=True),
        lax.all_gather(text_mod_total.astype(jnp.bfloat16), "fsdp", axis=0, tiled=True),
    )
    image_mod_weight = jnp.einsum(
        "fr,flk->lrk", condition_slice, image_every, preferred_element_type=jnp.float32
    )
    text_mod_weight = jnp.einsum(
        "fr,flk->lrk", condition_slice, text_every, preferred_element_type=jnp.float32
    )
    condition_parts = jnp.einsum(
        "flk,lrk->fr", image_every, image_modulator, preferred_element_type=jnp.float32
    ) + jnp.einsum("flk,lrk->fr", text_every, text_modulator, preferred_element_type=jnp.float32)
    silu_grad = lax.all_to_all(condition_parts, "fsdp", split_axis=0, concat_axis=1, tiled=True)
    sigmoid_value = jax.nn.sigmoid(condition_value)
    condition_grad = silu_grad * sigmoid_value * (1.0 + condition_value * (1.0 - sigmoid_value))

    def stacked_grad(position):
        return jnp.stack([weight_grads[0][position]])

    return (
        (occupancy * hidden[0])[None].astype(jnp.bfloat16),
        (occupancy * hidden[1])[None].astype(jnp.bfloat16),
        flowing[0][None].astype(jnp.bfloat16),
        flowing[1][None].astype(jnp.bfloat16),
        condition_grad,
        image_mod_weight,
        stacked_grad(0),
        stacked_grad(1),
        stacked_grad(2),
        stacked_grad(3),
        text_mod_weight,
        stacked_grad(4),
        stacked_grad(5),
        stacked_grad(6),
        stacked_grad(7),
    )


def solution(mesh):
    placed = (
        P("fsdp", "seq", None),
        P("fsdp", "seq", None),
        P("fsdp", None),
        P("fsdp"),
        P("fsdp", "seq", None),
        P("fsdp", "seq", None),
        P(None, "fsdp", None),
        P(None, "fsdp", None),
        P(None, "fsdp", None),
        P(None, "fsdp", None),
        P(None, "fsdp", None),
        P(None, "fsdp", None),
        P(None, "fsdp", None),
        P(None, "fsdp", None),
        P(None, "fsdp", None),
        P(None, "fsdp", None),
    )
    return jax.shard_map(
        per_device,
        mesh=mesh,
        in_specs=placed,
        out_specs=(
            P("fsdp", "seq", None),
            P("fsdp", "seq", None),
            P("fsdp", "seq", None),
            P("fsdp", "seq", None),
            P("fsdp", None),
            P(None, "fsdp", None),
            P(None, "fsdp", None),
            P(None, "fsdp", None),
            P(None, "fsdp", None),
            P(None, "fsdp", None),
            P(None, "fsdp", None),
            P(None, "fsdp", None),
            P(None, "fsdp", None),
            P(None, "fsdp", None),
            P(None, "fsdp", None),
        ),
        check_vma=False,
    )
```

profile of v0, /device:TPU:0, one launch (start us, length us, event | category | flops | bytes accessed | tf_op | source)
XLA Modules:
  0.0 4345.3 jit_solution(4088864998627911147)
XLA Ops:
  8.7 34.1 all-gather.8
  59.7 61.1 %all-reduce.8.cloned.1.call-done = (f32[8,1,9216]{2,0,1:T(8,128)}, f32[8,1,9216]{2,0,1:T(8,128)}) async-done(((f32[8,1,9216]{2,0,1:T(8,128)}, f32[8,1,9216]{2,0,1:T(8,128)}), (f32[8,1,9216]{2,0,1:T(8,128)}, f32[8,1,9216]{2,0,1:T(8,128)})) %all-reduce.8.cloned.1.call-update) | async-done | bytes 589840
  125.6 191.9 %all-gather.20.cloned.1.call-done = bf16[1,1536,4608]{2,1,0:T(8,128)(2,1)} async-done(((bf16[1,192,4608]{2,1,0:T(8,128)(2,1)}), bf16[1,1536,4608]{2,1,0:T(8,128)(2,1)}) %all-gather.20.cloned.1.call-update) | async-done | bytes 14155792 | tf_op jit(solution)/shard_map/all_gather | solution.py:54
  317.5 8.5 fusion.81
  326.0 187.2 %all-gather.18.cloned.1.call-done = bf16[1,1536,4608]{2,1,0:T(8,128)(2,1)} async-done(((bf16[1,192,4608]{2,1,0:T(8,128)(2,1)}), bf16[1,1536,4608]{2,1,0:T(8,128)(2,1)}) %all-gather.18.cloned.1.call-update) | async-done | bytes 14155792 | tf_op jit(solution)/shard_map/all_gather | solution.py:50
  513.2 9.3 fusion.71
  524.2 5.6 reshape.488
  538.4 32.5 all-to-all-done
  570.8 7.3 copy.63
  578.1 6.4 reshape.489
  595.8 37.9 while.26
  648.4 11.9 all-to-all-done.1
  669.9 5.4 fusion.211
  677.4 277.6 %all-gather.24.cloned.1.call-done = bf16[1,1536,6144]{2,1,0:T(8,128)(2,1)} async-done(((bf16[1,192,6144]{2,1,0:T(8,128)(2,1)}), bf16[1,1536,6144]{2,1,0:T(8,128)(2,1)}) %all-gather.24.cloned.1.call-update) | async-done | bytes 18874384 | tf_op jit(solution)/shard_map/all_gather | solution.py:52
  955.0 11.3 fusion.61
  966.2 352.5 %all-gather.26.cloned.1.call-done = bf16[1,6144,1536]{2,1,0:T(8,128)(2,1)} async-done(((bf16[1,768,1536]{2,1,0:T(8,128)(2,1)}), bf16[1,6144,1536]{2,1,0:T(8,128)(2,1)}) %all-gather.26.cloned.1.call-update) | async-done | bytes 18874384 | tf_op jit(solution)/shard_map/all_gather | solution.py:53
  1318.7 13.7 fusion.80
  1332.5 11.4 multiply_reduce_fusion.1
  1343.9 15.7 fusion.128
  1366.0 34.2 all-gather.28.cloned.1.call-done
  1405.8 356.8 %all-gather.30.cloned.1.call-done = bf16[1,1536,6144]{2,1,0:T(8,128)(2,1)} async-done(((bf16[1,192,6144]{2,1,0:T(8,128)(2,1)}), bf16[1,1536,6144]{2,1,0:T(8,128)(2,1)}) %all-gather.30.cloned.1.call-update) | async-done | bytes 18874384 | tf_op jit(solution)/shard_map/all_gather | solution.py:56
  1762.6 10.9 fusion.53
  1773.5 353.1 %all-gather.32.cloned.1.call-done = bf16[1,6144,1536]{2,1,0:T(8,128)(2,1)} async-done(((bf16[1,768,1536]{2,1,0:T(8,128)(2,1)}), bf16[1,6144,1536]{2,1,0:T(8,128)(2,1)}) %all-gather.32.cloned.1.call-update) | async-done | bytes 18874384 | tf_op jit(solution)/shard_map/all_gather | solution.py:57
  2126.6 13.2 fusion.141
  2139.8 13.7 multiply_reduce_fusion.7
  2154.2 11.8 fusion.181
  2183.9 8.2 all-to-all-done.2
  2198.5 82.7 %while.27 = (s32[]{:T(128)}, bf16[6,1184,64]{1,2,0:T(8,128)(2,1)}, bf16[6,1184,64]{1,2,0:T(8,128)(2,1)}, bf16[6,1184,64]{1,2,0:T(8,128)(2,1)}, bf16[6,1184,64]{2...) while((s32[]{:T(128)}, bf16[6,1184,64]{1,2,0:T(8,128)(2,1)}, ...), condition=%wide.region_20.21_spmd, body=%wide.region_18.20_spmd.sunk | while | flops 908553088 | bytes 44910832 | solution.py:262
  2284.9 7.7 copy.76
  2292.7 45.9 %all_to_all.76 = bf16[1184,3,1,384]{3,1,2,0:T(4,128)(2,1)S(1)} all-to-all(bf16[1184,3,1,384]{3,1,2,0:T(4,128)(2,1)} %copy.76), channel_id=1, replica_groups=mesh['seq'=4,'fsdp'=8] {'seq'}, dimensions={0} | all-to-all | bytes 5455872 | tf_op jit(solution)/shard_map/all_to_all | solution.py:269
  2346.5 11.1 convolution_convert_fusion.5
  2361.6 10.1 convolution_convert_fusion.4
  2371.8 11.3 convolution_convert_fusion.3
  2383.1 12.6 convolution_convert_fusion.2
  2396.0 10.3 convolution_convert_fusion.1
  2407.0 10.8 convolution_convert_fusion
  2418.4 10.9 fusion.174
  2430.0 156.3 %reduce-scatter.11.cloned.1.call-done = bf16[192,4608]{1,0:T(8,128)(2,1)} async-done(((bf16[1536,4608]{1,0:T(8,128)(2,1)}), bf16[192,4608]{1,0:T(8,128)(2,1)}) %reduce-scatter.11.cloned.1.call-update) | async-done | bytes 1769488 | tf_op jit(solution)/shard_map/reduce_scatter | solution.py:43
  2586.3 232.2 %reduce-scatter.19.cloned.1.call-done = bf16[192,4608]{1,0:T(8,128)(2,1)} async-done(((bf16[1536,4608]{1,0:T(8,128)(2,1)}), bf16[192,4608]{1,0:T(8,128)(2,1)}) %reduce-scatter.19.cloned.1.call-update) | async-done | bytes 1769488 | tf_op jit(solution)/shard_map/reduce_scatter | solution.py:43
  2818.5 312.6 %reduce-scatter.15.cloned.1.call-done = bf16[192,6144]{1,0:T(8,128)(2,1)} async-done(((bf16[1536,6144]{1,0:T(8,128)(2,1)}), bf16[192,6144]{1,0:T(8,128)(2,1)}) %reduce-scatter.15.cloned.1.call-update) | async-done | bytes 2359312 | tf_op jit(solution)/shard_map/reduce_scatter | solution.py:43
  3131.1 312.6 %reduce-scatter.17.cloned.1.call-done = bf16[768,1536]{1,0:T(8,128)(2,1)} async-done(((bf16[6144,1536]{1,0:T(8,128)(2,1)}), bf16[768,1536]{1,0:T(8,128)(2,1)}) %reduce-scatter.17.cloned.1.call-update) | async-done | bytes 2359312 | tf_op jit(solution)/shard_map/reduce_scatter | solution.py:43
  3443.7 312.6 %reduce-scatter.23.cloned.1.call-done = bf16[192,6144]{1,0:T(8,128)(2,1)} async-done(((bf16[1536,6144]{1,0:T(8,128)(2,1)}), bf16[192,6144]{1,0:T(8,128)(2,1)}) %reduce-scatter.23.cloned.1.call-update) | async-done | bytes 2359312 | tf_op jit(solution)/shard_map/reduce_scatter | solution.py:43
  3756.3 312.6 %reduce-scatter.25.cloned.1.call-done = bf16[768,1536]{1,0:T(8,128)(2,1)} async-done(((bf16[6144,1536]{1,0:T(8,128)(2,1)}), bf16[768,1536]{1,0:T(8,128)(2,1)}) %reduce-scatter.25.cloned.1.call-update) | async-done | bytes 2359312 | tf_op jit(solution)/shard_map/reduce_scatter | solution.py:43
  4069.6 11.7 fusion.121
  4087.9 16.0 all-reduce.3
  4103.9 31.3 all_gather.51
  4135.2 31.1 all_gather.50
  4187.0 131.6 %all-reduce.10.cloned.1.call-done = (bf16[1,192,4608]{2,1,0:T(8,128)(2,1)}, bf16[1,192,1536]{2,1,0:T(8,128)(2,1)}, bf16[1,192,6144]{2,1,0:T(8,128)(2,1)}, bf16[1...) async-done(((bf16[1,192,4608]{2,1,0:T(8,128)(2,1)}, ...) | async-done | bytes 14155792 | tf_op jit(solution)/shard_map/psum | solution.py:294
  (359 shorter events, 292.4 us)
Async XLA Ops:
  7.2 36.6 copy-start
  7.2 113.7 %all-reduce.8.cloned.1.call-start = ((), (), s32[]{:S(2)}) async-start(), calls=%async_computation.29 | async-start | bytes 1179648
  46.4 271.1 %all-gather.20.cloned.1.call-start = ((), (), s32[]{:S(2)}) async-start(), calls=%async_computation.22 | async-start | bytes 15925248 | tf_op jit(solution)/shard_map/all_gather | solution.py:54
  47.2 466.0 %all-gather.18.cloned.1.call-start = ((), (), s32[]{:S(2)}) async-start(), calls=%async_computation.21 | async-start | bytes 15925248 | tf_op jit(solution)/shard_map/all_gather | solution.py:50
  47.9 622.0 %all-gather.22.cloned.1.call-start = ((), (), s32[]{:S(2)}) async-start(), calls=%async_computation.23 | async-start | bytes 5308416 | tf_op jit(solution)/shard_map/all_gather | solution.py:51
  48.5 906.5 %all-gather.24.cloned.1.call-start = ((), (), s32[]{:S(2)}) async-start(), calls=%async_computation.24 | async-start | bytes 21233664 | tf_op jit(solution)/shard_map/all_gather | solution.py:52
  49.1 1269.7 %all-gather.26.cloned.1.call-start = ((), (), s32[]{:S(2)}) async-start(), calls=%async_computation.25 | async-start | bytes 21233664 | tf_op jit(solution)/shard_map/all_gather | solution.py:53
  49.7 1350.6 %all-gather.28.cloned.1.call-start = ((), (), s32[]{:S(2)}) async-start(), calls=%async_computation.26 | async-start | bytes 5308416 | tf_op jit(solution)/shard_map/all_gather | solution.py:55
  50.4 1712.2 %all-gather.30.cloned.1.call-start = ((), (), s32[]{:S(2)}) async-start(), calls=%async_computation.27 | async-start | bytes 21233664 | tf_op jit(solution)/shard_map/all_gather | solution.py:56
  51.2 2075.4 %all-gather.32.cloned.1.call-start = ((), (), s32[]{:S(2)}) async-start(), calls=%async_computation.28 | async-start | bytes 21233664 | tf_op jit(solution)/shard_map/all_gather | solution.py:57
  123.2 1220.6 %copy-start.35 = (f32[1536]{0:T(1024)}, f32[1536]{0:T(1024)S(1)}, u32[]{:S(2)}) copy-start(f32[1536]{0:T(1024)S(1)} %get-tuple-element.166) | copy-start | bytes 18436
  125.6 200.4 %copy-start.31 = (f32[1536]{0:T(1024)}, f32[1536]{0:T(1024)S(1)}, u32[]{:S(2)}) copy-start(f32[1536]{0:T(1024)S(1)} %get-tuple-element.163) | copy-start | bytes 18436
  533.5 37.3 all-to-all-start
  643.1 17.2 all-to-all-start.1
  647.3 1782.7 %reduce-scatter.13.cloned.1.call-start = ((), (), s32[]{:S(2)}) async-start(), calls=%async_computation.14 | async-start | bytes 5308416 | tf_op jit(solution)/shard_map/reduce_scatter | solution.py:43
  669.9 285.1 %copy-start.36 = (f32[1536]{0:T(1024)S(1)}, f32[1536]{0:T(1024)}, u32[]{:S(2)}) copy-start(f32[1536]{0:T(1024)} %get-tuple-element.170) | copy-start | bytes 18436
  1318.7 13.7 copy-start.5
  1318.7 13.7 copy-start.48
  1318.7 13.7 copy-start.56
  1332.5 11.4 copy-start.25
  1332.5 11.4 copy-start.63
  1343.9 16.8 copy-start.7
  1343.9 16.8 copy-start.44
  1364.3 35.9 copy-start.37
  1365.3 397.2 %copy-start.30 = (f32[1536]{0:T(1024)S(1)}, f32[1536]{0:T(1024)}, u32[]{:S(2)}) copy-start(f32[1536]{0:T(1024)} %get-tuple-element.160) | copy-start | bytes 18436
  1762.6 364.0 %copy-start.33 = (f32[1536]{0:T(1024)S(1)}, f32[1536]{0:T(1024)}, u32[]{:S(2)}) copy-start(f32[1536]{0:T(1024)} %get-tuple-element.159) | copy-start | bytes 18436
  2154.2 11.8 copy-start.38
  2174.9 17.2 all-to-all-start.2
  2179.1 250.9 %reduce-scatter.21.cloned.1.call-start = ((), (), s32[]{:S(2)}) async-start(), calls=%async_computation.18 | async-start | bytes 5308416 | tf_op jit(solution)/shard_map/reduce_scatter | solution.py:43
  2183.8 402.5 %reduce-scatter.11.cloned.1.call-start = ((), (), s32[]{:S(2)}) async-start(), calls=%async_computation.13 | async-start | bytes 15925248 | tf_op jit(solution)/shard_map/reduce_scatter | solution.py:43
  2357.6 460.9 %reduce-scatter.19.cloned.1.call-start = ((), (), s32[]{:S(2)}) async-start(), calls=%async_computation.17 | async-start | bytes 15925248 | tf_op jit(solution)/shard_map/reduce_scatter | solution.py:43
  2371.7 759.4 %reduce-scatter.15.cloned.1.call-start = ((), (), s32[]{:S(2)}) async-start(), calls=%async_computation.15 | async-start | bytes 21233664 | tf_op jit(solution)/shard_map/reduce_scatter | solution.py:43
  2383.1 1060.7 %reduce-scatter.17.cloned.1.call-start = ((), (), s32[]{:S(2)}) async-start(), calls=%async_computation.16 | async-start | bytes 21233664 | tf_op jit(solution)/shard_map/reduce_scatter | solution.py:43
  2395.7 1360.5 %reduce-scatter.23.cloned.1.call-start = ((), (), s32[]{:S(2)}) async-start(), calls=%async_computation.19 | async-start | bytes 21233664 | tf_op jit(solution)/shard_map/reduce_scatter | solution.py:43
  2406.3 1662.6 %reduce-scatter.25.cloned.1.call-start = ((), (), s32[]{:S(2)}) async-start(), calls=%async_computation.20 | async-start | bytes 21233664 | tf_op jit(solution)/shard_map/reduce_scatter | solution.py:43
  2417.8 1900.8 %all-reduce.10.cloned.1.call-start = ((), (), s32[]{:S(2)}) async-start(), calls=%async_computation.30 | async-start | bytes 28311552 | tf_op jit(solution)/shard_map/psum | solution.py:294
  4069.6 12.3 copy-start.61
  4069.6 12.9 copy-start.60
  4069.6 13.5 copy-start.58
  4069.6 14.1 copy-start.57
  4069.6 14.7 copy-start.59
  4069.6 15.9 copy-start.67
  4069.6 16.5 copy-start.65
  4069.6 17.1 copy-start.64
  4069.6 17.7 copy-start.66
  4103.9 63.4 %copy-start.3 = (bf16[1,192,9216]{2,1,0:T(8,128)(2,1)S(1)}, bf16[1,192,9216]{2,1,0:T(8,128)(2,1)}, u32[]{:S(2)}) copy-start(bf16[1,192,9216]{2,1,0:T(8,128)(2,1)} %param.26) | copy-start | bytes 10616836
  4135.2 33.2 copy-start.21
  4169.0 15.9 all-to-all-start.4
  (48 other events, 177.4 us)
Sparse Core Ops, SparseCore 0:
  46.5 74.3 all-reduce.7
  123.1 194.3 all-gather.19
  319.7 193.4 all-gather.17
  515.2 77.4 all-gather.21
  594.2 360.7 all-gather.23
  956.3 362.3 all-gather.25
  1320.9 79.2 all-gather.27
  1401.8 360.7 all-gather.29
  1764.1 362.4 all-gather.31
  2130.6 95.6 reduce-scatter.12
  2230.5 95.2 reduce-scatter.20
  2357.7 228.6 reduce-scatter.10
  2590.0 228.4 reduce-scatter.18
  2822.2 308.8 reduce-scatter.14
  3134.8 308.8 reduce-scatter.16
  3447.4 308.7 reduce-scatter.22
  3760.0 308.8 reduce-scatter.24
  4071.9 246.6 all-reduce.9
where the time goes:
time: 4360 us; the launch traced here: 4350 us
  waiting for transfers between devices  3640 us (83%)
  matrix products  349 us (8%)
  blocking collectives  158 us (4%)
  local copies, waits for them, and re-layouts  102 us (2%)
  other arithmetic  58 us (1%)
    reduce_scatter x8, waiting for transfers between devices, reduce_rows(): lax.psum_scatter(product_tn(former, latter).astype(jnp.bfloat16), 'fsdp',...  1640 us
    all_gather x1, waiting for transfers between devices, collect(): lax.all_gather(weights[6][layer_index], 'fsdp', axis=0, tiled=True)  357 us
    all_gather x1, waiting for transfers between devices, collect(): lax.all_gather(weights[7][layer_index], 'fsdp', axis=0, tiled=True)  353 us
    all_gather x1, waiting for transfers between devices, collect(): lax.all_gather(weights[3][layer_index], 'fsdp', axis=0, tiled=True)  353 us
    all_gather x1, waiting for transfers between devices, collect(): lax.all_gather(weights[2][layer_index], 'fsdp', axis=0, tiled=True)  278 us
    all_gather x1, waiting for transfers between devices, collect(): lax.all_gather(weights[4][layer_index], 'fsdp', axis=0, tiled=True)  192 us
    all_gather x1, waiting for transfers between devices, collect(): lax.all_gather(weights[0][layer_index], 'fsdp', axis=0, tiled=True)  187 us
    psum x1, waiting for transfers between devices, per_device(): lax.psum(terms[0].astype(jnp.bfloat16), 'seq').astype(jnp.float32)  132 us
  transfers between devices with their start and end apart: 22, of which 18 were waited for; matrix products, arithmetic and copies ran while one was open for 11% of the time, Pallas kernels for 0%

commit v1 on v0

--- a/solution.py
+++ b/solution.py
@@ -291,7 +291,9 @@
             )
         mod_grads[layer_index] = layer_mods
         weight_grads[layer_index] = (
-            lax.psum(terms[0].astype(jnp.bfloat16), "seq").astype(jnp.float32),
+            jnp.sum(lax.all_gather(terms[0].astype(jnp.bfloat16), "seq"), axis=0).astype(
+                jnp.float32
+            ),
             lax.psum(terms[1].astype(jnp.bfloat16), "seq").astype(jnp.float32),
             lax.psum(terms[2].astype(jnp.bfloat16), "seq").astype(jnp.float32),
             lax.psum(terms[3].astype(jnp.bfloat16), "seq").astype(jnp.float32),

time: 4360 us -> 4590 us (1.053)
  waiting for transfers between devices: 3640 us -> 3860 us
    reduce_scatter x8, waiting for transfers between devices: 1640 us -> 1810 us  [reduce_rows(): lax.psum_scatter(product_tn(former, latter).astype(jnp.bfloat16), 'fsdp',...]
    all_gather x1, waiting for transfers between devices: 278 us -> 349 us  [collect(): lax.all_gather(weights[2][layer_index], 'fsdp', axis=0, tiled=True)]
  transfers between devices with their start and end apart: 22 -> 23, of which waited for: 18 -> 19; matrix products, arithmetic and copies ran while one was open for 11% -> 7% of each run, Pallas kernels for 0% -> 0%
where the time goes in v1:
time: 4590 us; the launch traced here: 4580 us
  waiting for transfers between devices  3860 us (84%)
  matrix products  349 us (8%)
  blocking collectives  158 us (3%)
  local copies, waits for them, and re-layouts  106 us (2%)
  other arithmetic  68.2 us (1%)
    reduce_scatter x8, waiting for transfers between devices, reduce_rows(): lax.psum_scatter(product_tn(former, latter).astype(jnp.bfloat16), 'fsdp',...  1810 us
    all_gather x1, waiting for transfers between devices, collect(): lax.all_gather(weights[7][layer_index], 'fsdp', axis=0, tiled=True)  353 us
    all_gather x1, waiting for transfers between devices, collect(): lax.all_gather(weights[3][layer_index], 'fsdp', axis=0, tiled=True)  353 us
    all_gather x1, waiting for transfers between devices, collect(): lax.all_gather(weights[2][layer_index], 'fsdp', axis=0, tiled=True)  349 us
    all_gather x1, waiting for transfers between devices, collect(): lax.all_gather(weights[6][layer_index], 'fsdp', axis=0, tiled=True)  338 us
    all_gather x1, waiting for transfers between devices, collect(): lax.all_gather(weights[4][layer_index], 'fsdp', axis=0, tiled=True)  192 us
    all_gather x1, waiting for transfers between devices, collect(): lax.all_gather(weights[0][layer_index], 'fsdp', axis=0, tiled=True)  187 us
    psum x1, waiting for transfers between devices, per_device(): lax.psum(terms[1].astype(jnp.bfloat16), 'seq').astype(jnp.float32)  156 us
  transfers between devices with their start and end apart: 23, of which 19 were waited for; matrix products, arithmetic and copies ran while one was open for 7% of the time, Pallas kernels for 0%

profile of v1, /device:TPU:0, one launch (start us, length us, event | category | flops | bytes accessed | tf_op | source)
XLA Modules:
  0.0 4579.8 jit_solution(7084917821871566904)
XLA Ops:
  8.7 34.1 all-gather.9
  59.7 61.1 %all-reduce.8.cloned.1.call-done = (f32[8,1,9216]{2,0,1:T(8,128)}, f32[8,1,9216]{2,0,1:T(8,128)}) async-done(((f32[8,1,9216]{2,0,1:T(8,128)}, f32[8,1,9216]{2,0,1:T(8,128)}), (f32[8,1,9216]{2,0,1:T(8,128)}, f32[8,1,9216]{2,0,1:T(8,128)})) %all-reduce.8.cloned.1.call-update) | async-done | bytes 589840
  125.6 191.9 %all-gather.22.cloned.1.call-done = bf16[1,1536,4608]{2,1,0:T(8,128)(2,1)} async-done(((bf16[1,192,4608]{2,1,0:T(8,128)(2,1)}), bf16[1,1536,4608]{2,1,0:T(8,128)(2,1)}) %all-gather.22.cloned.1.call-update) | async-done | bytes 14155792 | tf_op jit(solution)/shard_map/all_gather | solution.py:54
  317.5 8.5 fusion.81
  326.0 187.2 %all-gather.20.cloned.1.call-done = bf16[1,1536,4608]{2,1,0:T(8,128)(2,1)} async-done(((bf16[1,192,4608]{2,1,0:T(8,128)(2,1)}), bf16[1,1536,4608]{2,1,0:T(8,128)(2,1)}) %all-gather.20.cloned.1.call-update) | async-done | bytes 14155792 | tf_op jit(solution)/shard_map/all_gather | solution.py:50
  513.2 9.3 fusion.71
  538.4 32.5 all-to-all-done
  570.8 7.3 copy.63
  578.1 6.4 reshape.498
  595.8 37.9 while.26
  648.4 12.3 all-to-all-done.1
  685.8 348.9 %all-gather.26.cloned.1.call-done = bf16[1,1536,6144]{2,1,0:T(8,128)(2,1)} async-done(((bf16[1,192,6144]{2,1,0:T(8,128)(2,1)}), bf16[1,1536,6144]{2,1,0:T(8,128)(2,1)}) %all-gather.26.cloned.1.call-update) | async-done | bytes 18874384 | tf_op jit(solution)/shard_map/all_gather | solution.py:52
  1034.7 11.2 fusion.61
  1045.9 352.7 %all-gather.28.cloned.1.call-done = bf16[1,6144,1536]{2,1,0:T(8,128)(2,1)} async-done(((bf16[1,768,1536]{2,1,0:T(8,128)(2,1)}), bf16[1,6144,1536]{2,1,0:T(8,128)(2,1)}) %all-gather.28.cloned.1.call-update) | async-done | bytes 18874384 | tf_op jit(solution)/shard_map/all_gather | solution.py:53
  1398.6 13.8 fusion.80
  1412.5 11.9 multiply_reduce_fusion.1
  1425.0 337.6 %all-gather.32.cloned.1.call-done = bf16[1,1536,6144]{2,1,0:T(8,128)(2,1)} async-done(((bf16[1,192,6144]{2,1,0:T(8,128)(2,1)}), bf16[1,1536,6144]{2,1,0:T(8,128)(2,1)}) %all-gather.32.cloned.1.call-update) | async-done | bytes 18874384 | tf_op jit(solution)/shard_map/all_gather | solution.py:56
  1762.6 10.9 fusion.53
  1773.5 353.0 %all-gather.34.cloned.1.call-done = bf16[1,6144,1536]{2,1,0:T(8,128)(2,1)} async-done(((bf16[1,768,1536]{2,1,0:T(8,128)(2,1)}), bf16[1,6144,1536]{2,1,0:T(8,128)(2,1)}) %all-gather.34.cloned.1.call-update) | async-done | bytes 18874384 | tf_op jit(solution)/shard_map/all_gather | solution.py:57
  2126.5 13.1 fusion.141
  2139.6 13.6 multiply_reduce_fusion.7
  2153.9 11.7 fusion.181
  2169.7 15.6 fusion.128
  2192.2 12.9 all-to-all-done.2
  2211.6 82.6 %while.27 = (s32[]{:T(128)}, bf16[6,1184,64]{1,2,0:T(8,128)(2,1)}, bf16[6,1184,64]{1,2,0:T(8,128)(2,1)}, bf16[6,1184,64]{1,2,0:T(8,128)(2,1)}, bf16[6,1184,64]{2...) while((s32[]{:T(128)}, bf16[6,1184,64]{1,2,0:T(8,128)(2,1)}, ...), condition=%wide.region_20.21_spmd, body=%wide.region_18.20_spmd.sunk | while | flops 908553088 | bytes 44910832 | solution.py:262
  2297.9 7.7 copy.76
  2305.7 45.9 %all_to_all.76 = bf16[1184,3,1,384]{3,1,2,0:T(4,128)(2,1)S(1)} all-to-all(bf16[1184,3,1,384]{3,1,2,0:T(4,128)(2,1)} %copy.76), channel_id=1, replica_groups=mesh['seq'=4,'fsdp'=8] {'seq'}, dimensions={0} | all-to-all | bytes 5455872 | tf_op jit(solution)/shard_map/all_to_all | solution.py:269
  2359.4 11.1 convolution_convert_fusion.5
  2385.8 10.1 convolution_convert_fusion.4
  2395.9 11.7 convolution_convert_fusion.3
  2408.3 12.6 convolution_convert_fusion.2
  2421.6 10.5 convolution_convert_fusion.1
  2432.8 10.6 convolution_convert_fusion
  2443.5 155.7 %reduce-scatter.11.cloned.1.call-done = bf16[192,4608]{1,0:T(8,128)(2,1)} async-done(((bf16[1536,4608]{1,0:T(8,128)(2,1)}), bf16[192,4608]{1,0:T(8,128)(2,1)}) %reduce-scatter.11.cloned.1.call-update) | async-done | bytes 1769488 | tf_op jit(solution)/shard_map/reduce_scatter | solution.py:43
  2599.5 10.8 fusion.174
  2610.9 10.9 fusion.121
  2624.3 74.0 %reduce-scatter.13.cloned.1.call-done = bf16[192,1536]{1,0:T(8,128)(2,1)} async-done(((bf16[1536,1536]{1,0:T(8,128)(2,1)}), bf16[192,1536]{1,0:T(8,128)(2,1)}) %reduce-scatter.13.cloned.1.call-update) | async-done | bytes 589840 | tf_op jit(solution)/shard_map/reduce_scatter | solution.py:43
  2698.2 99.4 %reduce-scatter.21.cloned.1.call-done = bf16[192,1536]{1,0:T(8,128)(2,1)} async-done(((bf16[1536,1536]{1,0:T(8,128)(2,1)}), bf16[192,1536]{1,0:T(8,128)(2,1)}) %reduce-scatter.21.cloned.1.call-update) | async-done | bytes 589840 | tf_op jit(solution)/shard_map/reduce_scatter | solution.py:43
  2797.6 232.7 %reduce-scatter.19.cloned.1.call-done = bf16[192,4608]{1,0:T(8,128)(2,1)} async-done(((bf16[1536,4608]{1,0:T(8,128)(2,1)}), bf16[192,4608]{1,0:T(8,128)(2,1)}) %reduce-scatter.19.cloned.1.call-update) | async-done | bytes 1769488 | tf_op jit(solution)/shard_map/reduce_scatter | solution.py:43
  3030.3 312.7 %reduce-scatter.15.cloned.1.call-done = bf16[192,6144]{1,0:T(8,128)(2,1)} async-done(((bf16[1536,6144]{1,0:T(8,128)(2,1)}), bf16[192,6144]{1,0:T(8,128)(2,1)}) %reduce-scatter.15.cloned.1.call-update) | async-done | bytes 2359312 | tf_op jit(solution)/shard_map/reduce_scatter | solution.py:43
  3343.0 312.6 %reduce-scatter.17.cloned.1.call-done = bf16[768,1536]{1,0:T(8,128)(2,1)} async-done(((bf16[6144,1536]{1,0:T(8,128)(2,1)}), bf16[768,1536]{1,0:T(8,128)(2,1)}) %reduce-scatter.17.cloned.1.call-update) | async-done | bytes 2359312 | tf_op jit(solution)/shard_map/reduce_scatter | solution.py:43
  3655.6 312.5 %reduce-scatter.23.cloned.1.call-done = bf16[192,6144]{1,0:T(8,128)(2,1)} async-done(((bf16[1536,6144]{1,0:T(8,128)(2,1)}), bf16[192,6144]{1,0:T(8,128)(2,1)}) %reduce-scatter.23.cloned.1.call-update) | async-done | bytes 2359312 | tf_op jit(solution)/shard_map/reduce_scatter | solution.py:43
  3968.2 312.6 %reduce-scatter.25.cloned.1.call-done = bf16[768,1536]{1,0:T(8,128)(2,1)} async-done(((bf16[6144,1536]{1,0:T(8,128)(2,1)}), bf16[768,1536]{1,0:T(8,128)(2,1)}) %reduce-scatter.25.cloned.1.call-update) | async-done | bytes 2359312 | tf_op jit(solution)/shard_map/reduce_scatter | solution.py:43
  4289.7 15.8 all-reduce.3
  4305.5 31.2 all_gather.57
  4336.7 31.2 all_gather.56
  4388.8 6.0 reduce_sum.310
  4398.8 155.5 %all-reduce.10.cloned.1.call-done = (bf16[1,192,1536]{2,1,0:T(8,128)(2,1)}, bf16[1,192,6144]{2,1,0:T(8,128)(2,1)}, bf16[1,768,1536]{2,1,0:T(8,128)(2,1)}, bf16[1...) async-done(((bf16[1,192,1536]{2,1,0:T(8,128)(2,1)}, bf16[1,192,6144]{2,1,0:T(8,128)(2,1)}, ...) | async-done | bytes 12386320 | tf_op jit(solution)/shard_map/psum | solution.py:297
  (368 shorter events, 312.5 us)
Async XLA Ops:
  7.2 36.6 copy-start
  7.2 113.7 %all-reduce.8.cloned.1.call-start = ((), (), s32[]{:S(2)}) async-start(), calls=%async_computation.30 | async-start | bytes 1179648
  46.4 271.1 %all-gather.22.cloned.1.call-start = ((), (), s32[]{:S(2)}) async-start(), calls=%async_computation.22 | async-start | bytes 15925248 | tf_op jit(solution)/shard_map/all_gather | solution.py:54
  47.2 466.0 %all-gather.20.cloned.1.call-start = ((), (), s32[]{:S(2)}) async-start(), calls=%async_computation.21 | async-start | bytes 15925248 | tf_op jit(solution)/shard_map/all_gather | solution.py:50
  47.9 623.8 %all-gather.30.cloned.1.call-start = ((), (), s32[]{:S(2)}) async-start(), calls=%async_computation.26 | async-start | bytes 5308416 | tf_op jit(solution)/shard_map/all_gather | solution.py:55
  48.5 628.7 %all-gather.24.cloned.1.call-start = ((), (), s32[]{:S(2)}) async-start(), calls=%async_computation.23 | async-start | bytes 5308416 | tf_op jit(solution)/shard_map/all_gather | solution.py:51
  49.1 985.6 %all-gather.26.cloned.1.call-start = ((), (), s32[]{:S(2)}) async-start(), calls=%async_computation.24 | async-start | bytes 21233664 | tf_op jit(solution)/shard_map/all_gather | solution.py:52
  49.7 1349.0 %all-gather.28.cloned.1.call-start = ((), (), s32[]{:S(2)}) async-start(), calls=%async_computation.25 | async-start | bytes 21233664 | tf_op jit(solution)/shard_map/all_gather | solution.py:53
  50.4 1712.2 %all-gather.32.cloned.1.call-start = ((), (), s32[]{:S(2)}) async-start(), calls=%async_computation.27 | async-start | bytes 21233664 | tf_op jit(solution)/shard_map/all_gather | solution.py:56
  51.2 2075.4 %all-gather.34.cloned.1.call-start = ((), (), s32[]{:S(2)}) async-start(), calls=%async_computation.28 | async-start | bytes 21233664 | tf_op jit(solution)/shard_map/all_gather | solution.py:57
  123.3 1289.2 %copy-start.34 = (f32[1536]{0:T(1024)}, f32[1536]{0:T(1024)S(1)}, u32[]{:S(2)}) copy-start(f32[1536]{0:T(1024)S(1)} %get-tuple-element.166) | copy-start | bytes 18436
  125.6 200.3 %copy-start.30 = (f32[1536]{0:T(1024)}, f32[1536]{0:T(1024)S(1)}, u32[]{:S(2)}) copy-start(f32[1536]{0:T(1024)S(1)} %get-tuple-element.163) | copy-start | bytes 18436
  513.2 9.3 copy-start.25
  533.5 37.3 all-to-all-start
  643.1 17.6 all-to-all-start.1
  677.2 7.4 copy-start.70
  677.2 357.5 %copy-start.36 = (f32[1536]{0:T(1024)S(1)}, f32[1536]{0:T(1024)}, u32[]{:S(2)}) copy-start(f32[1536]{0:T(1024)} %get-tuple-element.170) | copy-start | bytes 18436
  1398.6 13.8 copy-start.6
  1398.6 13.8 copy-start.48
  1398.6 13.8 copy-start.56
  1412.5 350.1 %copy-start.28 = (f32[1536]{0:T(1024)S(1)}, f32[1536]{0:T(1024)}, u32[]{:S(2)}) copy-start(f32[1536]{0:T(1024)} %get-tuple-element.160) | copy-start | bytes 18436
  1762.6 363.9 %copy-start.32 = (f32[1536]{0:T(1024)S(1)}, f32[1536]{0:T(1024)}, u32[]{:S(2)}) copy-start(f32[1536]{0:T(1024)} %get-tuple-element.159) | copy-start | bytes 18436
  2153.9 11.7 copy-start.38
  2153.9 15.7 copy-start.73
  2165.6 19.8 slice-start
  2169.7 15.7 slice-start.1
  2169.7 15.7 copy-start.44
  2187.9 17.2 all-to-all-start.2
  2192.2 407.0 %reduce-scatter.11.cloned.1.call-start = ((), (), s32[]{:S(2)}) async-start(), calls=%async_computation.13 | async-start | bytes 15925248 | tf_op jit(solution)/shard_map/reduce_scatter | solution.py:43
  2370.5 327.7 %reduce-scatter.13.cloned.1.call-start = ((), (), s32[]{:S(2)}) async-start(), calls=%async_computation.14 | async-start | bytes 5308416 | tf_op jit(solution)/shard_map/reduce_scatter | solution.py:43
  2376.5 421.2 %reduce-scatter.21.cloned.1.call-start = ((), (), s32[]{:S(2)}) async-start(), calls=%async_computation.18 | async-start | bytes 5308416 | tf_op jit(solution)/shard_map/reduce_scatter | solution.py:43
  2381.9 648.4 %reduce-scatter.19.cloned.1.call-start = ((), (), s32[]{:S(2)}) async-start(), calls=%async_computation.17 | async-start | bytes 15925248 | tf_op jit(solution)/shard_map/reduce_scatter | solution.py:43
  2395.9 947.1 %reduce-scatter.15.cloned.1.call-start = ((), (), s32[]{:S(2)}) async-start(), calls=%async_computation.15 | async-start | bytes 21233664 | tf_op jit(solution)/shard_map/reduce_scatter | solution.py:43
  2407.7 1247.9 %reduce-scatter.17.cloned.1.call-start = ((), (), s32[]{:S(2)}) async-start(), calls=%async_computation.16 | async-start | bytes 21233664 | tf_op jit(solution)/shard_map/reduce_scatter | solution.py:43
  2421.0 1547.2 %reduce-scatter.23.cloned.1.call-start = ((), (), s32[]{:S(2)}) async-start(), calls=%async_computation.19 | async-start | bytes 21233664 | tf_op jit(solution)/shard_map/reduce_scatter | solution.py:43
  2432.1 1848.6 %reduce-scatter.25.cloned.1.call-start = ((), (), s32[]{:S(2)}) async-start(), calls=%async_computation.20 | async-start | bytes 21233664 | tf_op jit(solution)/shard_map/reduce_scatter | solution.py:43
  2443.4 1945.4 %all-gather.36.cloned.1.call-start = ((), (), s32[]{:S(2)}) async-start(), calls=%async_computation.29 | async-start | bytes 8847360 | tf_op jit(solution)/shard_map/all_gather | solution.py:294
  2599.2 11.7 copy-start.41
  2599.2 1955.2 %all-reduce.10.cloned.1.call-start = ((), (), s32[]{:S(2)}) async-start(), calls=%async_computation.31 | async-start | bytes 24772608 | tf_op jit(solution)/shard_map/psum | solution.py:297
  2599.5 11.4 copy-start.1
  2599.5 11.4 copy-start.10
  2599.5 11.4 copy-start.51
  2599.5 11.4 copy-start.60
  2610.9 12.1 copy-start.59
  2610.9 12.7 copy-start.58
  4305.5 63.3 %copy-start.4 = (bf16[1,192,9216]{2,1,0:T(8,128)(2,1)S(1)}, bf16[1,192,9216]{2,1,0:T(8,128)(2,1)}, u32[]{:S(2)}) copy-start(bf16[1,192,9216]{2,1,0:T(8,128)(2,1)} %param.26) | copy-start | bytes 10616836
  4336.7 33.2 copy-start.20
  4370.5 16.1 all-to-all-start.4
  (51 other events, 175.7 us)
Sparse Core Ops, SparseCore 0:
  46.5 74.3 all-reduce.7
  123.1 194.3 all-gather.21
  319.7 193.4 all-gather.19
  515.2 77.4 all-gather.29
  594.8 77.6 all-gather.23
  673.9 360.7 all-gather.25
  1036.2 362.3 all-gather.27
  1400.2 362.3 all-gather.31
  1764.1 362.3 all-gather.33
  2370.6 228.4 reduce-scatter.10
  2603.4 94.8 reduce-scatter.12
  2702.3 95.2 reduce-scatter.20
  2801.3 229.0 reduce-scatter.18
  3034.1 308.8 reduce-scatter.14
  3346.7 308.8 reduce-scatter.16
  3659.3 308.7 reduce-scatter.22
  3971.9 308.8 reduce-scatter.24
  4282.2 51.2 all-gather.35
  4336.7 217.5 all-reduce.9
